TPU v7x, 128 devices: a whole 4x4x4 slice. The times are simulated.
128 devices in a mesh: brick: 8 (over y, core), grp: 16 (over x, z).
Axes of the slice: x: 4, y: 4, z: 4, core: 2. Of those that a mesh axis runs over, the one named last changes fastest.
Arguments:
- source: float32 [16, 8, 2, 32, 1024], P('grp', 'brick'), may hold values from -21 to 21
- uptake: float32 [16, 8, 2, 32, 1024], P('grp', 'brick'), may hold values from 0.00015 to 0.006
- conductance: float32 [16, 8, 6, 2, 32, 1024], P('grp', 'brick'), may hold values from 0 to 3, as said below
- occupancy: int32 [16, 2, 8], replicated, may hold values from 0 to 1, as said below
- assignment: int32 [8], replicated, may hold values from 0 to 7, as said below
Outputs:
- solution_field: float32 [16, 8, 2, 32, 1024], P('grp', 'brick')
- residual: float32 [16, 8, 2, 32, 1024], P('grp', 'brick')
Inputs may be any that keep to these rules, and one draw needn't show every extreme that they name: `occupancy`: 1 marks an occupied brick; in every draw one patch of some slab has all its bricks occupied. `assignment`: each patch is held by exactly one index of brick. `conductance`: equal at both ends of a bond: the value toward +x at a cell is the value toward -x at its +x neighbour, likewise for y and z, the lattice being read cyclically; values toward +z and -z are 0.3 or more.
All inputs are finite; a program needn't handle non-finite values.
Results may differ from a plain program's by a relative error of at most 0.0003.
Values sent between devices are 32-bit elements; how exact they have to be, the bound alone decides.
A program may use at most 128 MiB of HBM per device.

v0:
```python
import jax
import jax.numpy as jnp
from jax import lax
from jax.sharding import PartitionSpec as P

BS = 32
PATCH_X = 1
PATCH_Y = 2
ITERS = 3
OMEGA = 0.6


def extended_2(block, sides, width):
    for axis, dim in sides:
        count = lax.axis_size(axis)
        forward = [(i, i + 1) for i in range(count - 1)]
        backward = [(target, source) for source, target in forward]
        low = lax.ppermute(
            lax.slice_in_dim(block, block.shape[dim] - width, None, axis=dim), axis, forward
        )
        high = lax.ppermute(lax.slice_in_dim(block, 0, width, axis=dim), axis, backward)
        block = jnp.concatenate([low, block, high], axis=dim)
    return block


def assemble(coarse_diag, couplings, strides):
    extent = coarse_diag.shape[0]
    matrix = jnp.diag(coarse_diag)
    for coupling, stride in zip(couplings, strides):
        banded = coupling[: extent - stride]
        matrix = matrix - jnp.diag(banded, stride) - jnp.diag(banded, -stride)
    return matrix


def pad_rows(block, capacity):
    return jnp.pad(block, ((0, capacity - block.shape[0]), (0, 0)))


def on_device(source, uptake, conductance, occupancy, assignment):
    face_size = BS * BS
    capacity = max(PATCH_X, PATCH_Y)
    slot_count = PATCH_X * PATCH_Y
    slab_index = lax.axis_index("grp")
    brick_index = lax.axis_index("brick")
    brick_count = lax.axis_size("brick")
    across = brick_count // 2
    peer_ids = jnp.arange(brick_count, dtype=jnp.int32)
    patch_index = assignment[brick_index]
    patch_row = patch_index // across
    patch_column = patch_index % across

    def owner_of(row_shift, column_shift):
        row_target = patch_row + row_shift
        column_target = patch_column + column_shift
        inside = (
            (row_target >= 0) & (row_target < 2) & (column_target >= 0) & (column_target < across)
        )
        holder = jnp.sum(jnp.where(assignment == row_target * across + column_target, peer_ids, 0))
        return jnp.where(inside, holder, -1)

    wanted = jnp.stack([owner_of(1, 0), owner_of(-1, 0), owner_of(0, 1), owner_of(0, -1)])
    padded = jnp.pad(occupancy, 1)
    window = lax.dynamic_slice(
        padded,
        (slab_index, patch_row * PATCH_X, patch_column * PATCH_Y),
        (3, PATCH_X + 2, PATCH_Y + 2),
    ).astype(jnp.float32)
    centre = window[1, 1:-1, 1:-1].reshape(slot_count)
    toward = [
        window[1, 2:, 1:-1],
        window[1, :-2, 1:-1],
        window[1, 1:-1, 2:],
        window[1, 1:-1, :-2],
        window[2, 1:-1, 1:-1],
        window[0, 1:-1, 1:-1],
    ]
    first_axis = lax.broadcasted_iota(jnp.int32, (1, BS, face_size), 1)
    flat_axis = lax.broadcasted_iota(jnp.int32, (1, BS, face_size), 2)
    second_axis = flat_axis // BS
    third_axis = flat_axis % BS
    cube_third = lax.broadcasted_iota(jnp.int32, (1, BS, BS, BS), 3)
    borders = [
        first_axis == BS - 1,
        first_axis == 0,
        second_axis == BS - 1,
        second_axis == 0,
        third_axis == BS - 1,
        third_axis == 0,
    ]
    bonds = conductance[0, 0]
    live_here = centre[:, None, None]
    effective = []
    for direction in range(6):
        neighbour_live = toward[direction].reshape(slot_count)[:, None, None]
        active = jnp.where(borders[direction], live_here * neighbour_live, live_here)
        effective.append(bonds[direction] * active)
    absorb = uptake[0, 0]
    diagonal = absorb
    for direction in range(6):
        diagonal = diagonal + effective[direction]

    def apply_operator(field):
        lower_x = field[:, 0, :]
        upper_x = field[:, BS - 1, :]
        lower_y = field[:, :, :BS].reshape(slot_count, face_size)
        upper_y = field[:, :, face_size - BS :].reshape(slot_count, face_size)
        cube = field.reshape(slot_count, BS, BS, BS)
        lower_z = cube[:, :, :, 0].reshape(slot_count, face_size)
        upper_z = cube[:, :, :, BS - 1].reshape(slot_count, face_size)
        grid_lower_x = lower_x.reshape(PATCH_X, PATCH_Y, face_size)
        grid_upper_x = upper_x.reshape(PATCH_X, PATCH_Y, face_size)
        grid_lower_y = lower_y.reshape(PATCH_X, PATCH_Y, face_size)
        grid_upper_y = upper_y.reshape(PATCH_X, PATCH_Y, face_size)
        outgoing_sides = jnp.stack(
            [
                pad_rows(grid_lower_x[0], capacity),
                pad_rows(grid_upper_x[PATCH_X - 1], capacity),
                pad_rows(grid_lower_y[:, 0], capacity),
                pad_rows(grid_upper_y[:, PATCH_Y - 1], capacity),
            ]
        )
        portion = lax.all_gather(outgoing_sides[None], "brick", axis=0, tiled=True)
        sources = jnp.arange(portion.shape[0], dtype=jnp.int32)
        matches = sources[:, None] == wanted[None, :]
        remote = jnp.zeros((4, capacity, face_size), jnp.float32) + jnp.sum(
            jnp.where(matches[:, :, None, None], portion, 0.0), axis=0
        )
        stacked = jnp.stack([lower_z, upper_z])
        extended = extended_2(stacked, (("grp", 0),), 1)
        from_below = extended[0].reshape(slot_count, BS, BS, 1)
        from_above = extended[3].reshape(slot_count, BS, BS, 1)
        beyond_xplus = jnp.concatenate(
            [grid_lower_x[1:], remote[0, :PATCH_Y][None]], axis=0
        ).reshape(slot_count, face_size)
        beyond_xminus = jnp.concatenate(
            [remote[1, :PATCH_Y][None], grid_upper_x[:-1]], axis=0
        ).reshape(slot_count, face_size)
        beyond_yplus = jnp.concatenate(
            [grid_lower_y[:, 1:], remote[2, :PATCH_X][:, None]], axis=1
        ).reshape(slot_count, BS, BS)
        beyond_yminus = jnp.concatenate(
            [remote[3, :PATCH_X][:, None], grid_upper_y[:, :-1]], axis=1
        ).reshape(slot_count, BS, BS)
        upper_neighbour = jnp.where(
            cube_third == BS - 1, from_above, jnp.roll(cube, -1, axis=3)
        ).reshape(slot_count, BS, face_size)
        lower_neighbour = jnp.where(cube_third == 0, from_below, jnp.roll(cube, 1, axis=3)).reshape(
            slot_count, BS, face_size
        )
        total = diagonal * field
        total = total - effective[0] * jnp.concatenate(
            [field[:, 1:, :], beyond_xplus[:, None, :]], axis=1
        )
        total = total - effective[1] * jnp.concatenate(
            [beyond_xminus[:, None, :], field[:, :-1, :]], axis=1
        )
        total = total - effective[2] * jnp.concatenate([field[:, :, BS:], beyond_yplus], axis=2)
        total = total - effective[3] * jnp.concatenate(
            [beyond_yminus, field[:, :, : face_size - BS]], axis=2
        )
        total = total - effective[4] * upper_neighbour
        total = total - effective[5] * lower_neighbour
        return total

    slot_ids = jnp.arange(slot_count)
    brick_first = slot_ids // PATCH_Y
    brick_second = slot_ids % PATCH_Y
    inside = [
        (brick_first < PATCH_X - 1).astype(jnp.float32),
        (brick_first > 0).astype(jnp.float32),
        (brick_second < PATCH_Y - 1).astype(jnp.float32),
        (brick_second > 0).astype(jnp.float32),
    ]
    face_sums = [
        jnp.sum(effective[0][:, BS - 1, :], axis=1),
        jnp.sum(effective[1][:, 0, :], axis=1),
        jnp.sum(effective[2][:, :, face_size - BS :], axis=(1, 2)),
        jnp.sum(effective[3][:, :, :BS], axis=(1, 2)),
        jnp.sum(effective[4].reshape(slot_count, BS, BS, BS)[:, :, :, BS - 1], axis=(1, 2)),
        jnp.sum(effective[5].reshape(slot_count, BS, BS, BS)[:, :, :, 0], axis=(1, 2)),
    ]
    coarse_diag = jnp.sum(absorb, axis=(1, 2))
    for direction in range(4):
        coarse_diag = coarse_diag + face_sums[direction] * inside[direction]
    coarse_diag = coarse_diag + face_sums[4] + face_sums[5]
    grp_count = lax.axis_size("grp")
    grp_ids = jnp.arange(grp_count, dtype=jnp.int32)

    def butterfly(values, axes):
        for axis in axes:
            count = lax.axis_size(axis)
            if count & count - 1:
                values = lax.psum(values, axis)
                continue
            stride = 1
            while stride < count:
                pairs = [(i, i ^ stride) for i in range(count)]
                values = values + lax.ppermute(values, axis, pairs)
                stride *= 2
        return values

    def slab_slot(values):
        here = (grp_ids == slab_index).astype(jnp.float32)
        return here[:, None, None] * values[None]

    forcing = source[0, 0] * live_here
    record = jnp.stack(
        [
            coarse_diag,
            face_sums[0] * inside[0],
            face_sums[2] * inside[2],
            face_sums[4],
            jnp.sum(forcing, axis=(1, 2)),
        ]
    )
    gathered = butterfly(slab_slot(record), ("grp",))
    columns = jnp.transpose(gathered, (1, 0, 2)).reshape(5, -1)
    matrix = assemble(columns[0], (columns[1], columns[2], columns[3]), (PATCH_Y, 1, slot_count))
    factor = jnp.linalg.cholesky(matrix)

    def coarse_solve(terms):
        middle = lax.linalg.triangular_solve(factor, terms[:, None], left_side=True, lower=True)
        result = lax.linalg.triangular_solve(
            factor, middle, left_side=True, lower=True, transpose_a=True
        )
        return lax.dynamic_slice_in_dim(result[:, 0], slab_index * slot_count, slot_count)

    def precondition(residual_field, terms):
        smoothed = OMEGA * residual_field / diagonal
        smoothed = smoothed + OMEGA * (residual_field - apply_operator(smoothed)) / diagonal
        return smoothed + coarse_solve(terms)[:, None, None]

    brick_here = (peer_ids == brick_index).astype(jnp.float32)

    def dot_and_sums(product, field):
        sums = slab_slot(jnp.sum(field, axis=(1, 2))[None])[:, 0]
        spread = brick_here[:, None, None] * sums[None]
        packed = jnp.concatenate([jnp.sum(product)[None], spread.reshape(-1)])
        total = butterfly(packed, ("brick", "grp"))
        mine = lax.dynamic_index_in_dim(
            total[1:].reshape(brick_count, -1), brick_index, keepdims=False
        )
        return (total[0], mine)

    def global_sum(values):
        return butterfly(jnp.sum(values)[None], ("brick", "grp"))[0]

    terms = columns[4]
    solution_field = jnp.zeros_like(forcing)
    residual = forcing
    search = precondition(residual, terms)
    energy = global_sum(residual * search)
    for iteration in range(ITERS):
        mapped = apply_operator(search)
        curvature, mapped_terms = dot_and_sums(search * mapped, mapped)
        step_size = energy / curvature
        solution_field = solution_field + step_size * search
        residual = residual - step_size * mapped
        if iteration + 1 < ITERS:
            terms = terms - step_size * mapped_terms
            smoothed = precondition(residual, terms)
            renewed = global_sum(residual * smoothed)
            search = smoothed + renewed / energy * search
            energy = renewed
    return (solution_field[None, None], residual[None, None])


def solution(mesh):
    return jax.shard_map(
        on_device,
        mesh=mesh,
        in_specs=(
            P("grp", "brick", None, None, None),
            P("grp", "brick", None, None, None),
            P("grp", "brick", None, None, None, None),
            P(),
            P(),
        ),
        out_specs=(P("grp", "brick", None, None, None), P("grp", "brick", None, None, None)),
        check_vma=False,
    )
```

profile of v0, /device:TPU:0, one launch (start us, length us, event | category | flops | bytes accessed | tf_op | source)
XLA Modules:
  0.0 795.7 jit_solution(16637626487733563843)
XLA Ops:
  31.3 5.5 multiply_divide_fusion.2
  62.5 13.4 %all-gather = f32[32,2,1024]{2,1,0:T(2,128)S(1)} all-gather(f32[4,2,1024]{2,1,0:T(2,128)S(1)} %copy.421), channel_id=2, replica_groups=mesh['brick'=8,'grp'=16] {'brick'}, dimensions={0}, use_global_device_ids=true | all-gather | bytes 294912 | tf_op jit(solution)/shard_map/all_gather | solution.py:122
  84.2 5.6 collective-permute-start.3
  121.3 8.5 %fusion.46 = (f32[2,32,32,32]{3,2,1,0:T(8,128)S(1)}, f32[2,32,32,32]{3,2,1,0:T(8,128)}, f32[2,32,32,32]{3,2,1,0:T(8,128)}) fusion(f32[2,32,32,32]{3,2,1,0:T(8,128)} %get-tuple-element.73, f32[2,32,32,32]{3,2,1,0:T(8,128)} %copy-done.15, f32[2,32,32,32]{3,2,1,0:T(8,128)} %copy-done.14, f32[2,32,32,32]{3,2,1,0:T(8,128)} %concatenate.668, ...), kind=kLoop, calls=%fused_computation.88 | loop fusion | flops 2293760 | bytes 4538480 | tf_op jit(solution)/shard_map/add | solution.py:231
  152.9 12.8 %all-gather.1 = f32[32,2,1024]{2,1,0:T(2,128)S(1)} all-gather(f32[4,2,1024]{2,1,0:T(2,128)S(1)} %copy.424), channel_id=3, replica_groups=mesh['brick'=8,'grp'=16] {'brick'}, dimensions={0}, use_global_device_ids=true | all-gather | bytes 294912 | tf_op jit(solution)/shard_map/all_gather | solution.py:122
  235.4 4.4 collective-permute-start.20
  296.8 13.2 %all-gather.2 = f32[32,2,1024]{2,1,0:T(2,128)S(1)} all-gather(f32[4,2,1024]{2,1,0:T(2,128)S(1)} %copy.430), channel_id=4, replica_groups=mesh['brick'=8,'grp'=16] {'brick'}, dimensions={0}, use_global_device_ids=true | all-gather | bytes 294912 | tf_op jit(solution)/shard_map/all_gather | solution.py:122
  315.7 6.9 multiply_divide_fusion.1
  391.8 4.0 collective-permute-start.27
  402.3 5.7 collective-permute-start.29
  408.8 4.9 collective-permute-start.30
  417.2 13.0 %all-gather.3 = f32[32,2,1024]{2,1,0:T(2,128)S(1)} all-gather(f32[4,2,1024]{2,1,0:T(2,128)S(1)} %copy.435), channel_id=5, replica_groups=mesh['brick'=8,'grp'=16] {'brick'}, dimensions={0}, use_global_device_ids=true | all-gather | bytes 294912 | tf_op jit(solution)/shard_map/all_gather | solution.py:122
  434.1 6.3 multiply_add_fusion.1
  486.5 4.1 collective-permute-start.37
  492.2 5.5 collective-permute-start.38
  517.4 13.1 %all-gather.4 = f32[32,2,1024]{2,1,0:T(2,128)S(1)} all-gather(f32[4,2,1024]{2,1,0:T(2,128)S(1)} %copy.440), channel_id=6, replica_groups=mesh['brick'=8,'grp'=16] {'brick'}, dimensions={0}, use_global_device_ids=true | all-gather | bytes 294912 | tf_op jit(solution)/shard_map/all_gather | solution.py:122
  535.4 6.6 multiply_divide_fusion
  608.9 4.0 collective-permute-start.45
  619.7 4.9 collective-permute-start.47
  625.6 4.0 collective-permute-start.48
  641.0 13.2 %all-gather.5 = f32[32,2,1024]{2,1,0:T(2,128)S(1)} all-gather(f32[4,2,1024]{2,1,0:T(2,128)S(1)} %copy.445), channel_id=7, replica_groups=mesh['brick'=8,'grp'=16] {'brick'}, dimensions={0}, use_global_device_ids=true | all-gather | bytes 294912 | tf_op jit(solution)/shard_map/all_gather | solution.py:122
  659.3 9.3 %multiply_add_fusion = f32[2,32,32,32]{3,2,1,0:T(8,128)S(1)} fusion(f32[2,32,32,32]{3,2,1,0:T(8,128)} %copy-done.16, f32[2,32,32,32]{3,2,1,0:T(8,128)} %get-tuple-element.73, f32[2,32,32,32]{3,2,1,0:T(8,128)} %copy-done.15, f32[2,32,32,32]{3,2,1,0:T(8,128)} %copy-done.14, f32[2,32,32,32]{3,2,1,0:T(8,128)} %concatenate.784, ...), kind=kLoop, calls=%fused_computation.76 | loop fusion | flops 3735552 | bytes 5865592 | tf_op jit(solution)/shard_map/add | solution.py:263
  740.0 3.9 fusion.96
  788.8 5.9 fusion.148
  (978 shorter events, 591.3 us)
Async XLA Ops:
  40.5 42.8 %collective-permute-start.2 = (f32[16,5,2]{2,0,1:T(8,128)}, f32[16,5,2]{2,0,1:T(8,128)}, u32[]{:S(2)}, u32[]{:S(2)}) collective-permute-start(f32[16,5,2]{2,0,1:T(8,128)} %broadcast_multiply_fusion.3), channel_id=1, source_target_pairs={{0,1},{1,0},{2,3},{3,2},{4,5},{5,4},{6,7},{7,6},{8,9},{9,8},{10,11... | collective-permute-start | bytes 1928 | tf_op jit(solution)/shard_map/ppermute | solution.py:198
  46.3 74.2 %collective-permute-start.1 = (f32[1,2,1024]{2,1,0:T(2,128)}, f32[1,2,1024]{2,1,0:T(2,128)}, u32[]{:S(2)}, u32[]{:S(2)}) collective-permute-start(f32[1,2,1024]{2,1,0:T(2,128)} %stack_reshape_squeeze.37), channel_id=1, source_target_pairs={{0,1},{1,2},{2,3},{3,4},{4,5},{5,6},{6,7},{7,8},{8,9},{9,10},{10,1... | collective-permute-start | bytes 24584 | tf_op jit(solution)/shard_map/ppermute | solution.py:18
  50.3 69.5 %collective-permute-start = (f32[1,2,1024]{2,1,0:T(2,128)}, f32[1,2,1024]{2,1,0:T(2,128)}, u32[]{:S(2)}, u32[]{:S(2)}) collective-permute-start(f32[1,2,1024]{2,1,0:T(2,128)} %stack_reshape_squeeze.36), channel_id=1, source_target_pairs={{1,0},{2,1},{3,2},{4,3},{5,4},{6,5},{7,6},{8,7},{9,8},{10,9},{11,1... | collective-permute-start | bytes 24584 | tf_op jit(solution)/shard_map/ppermute | solution.py:21
  84.2 7.6 collective-permute-start.3
  92.7 9.4 %collective-permute-start.4 = (f32[16,5,2]{2,0,1:T(8,128)S(1)}, f32[16,5,2]{2,0,1:T(8,128)S(1)}, u32[]{:S(2)}, u32[]{:S(2)}) collective-permute-start(f32[16,5,2]{2,0,1:T(8,128)S(1)} %fusion.258), channel_id=1, source_target_pairs={{0,4},{1,5},{2,6},{3,7},{4,0},{5,1},{6,2},{7,3},{8,12},{9,13},{10,... | collective-permute-start | bytes 1928 | tf_op jit(solution)/shard_map/ppermute | solution.py:198
  102.1 9.6 %collective-permute-start.5 = (f32[16,5,2]{2,0,1:T(8,128)S(1)}, f32[16,5,2]{2,0,1:T(8,128)S(1)}, u32[]{:S(2)}, u32[]{:S(2)}) collective-permute-start(f32[16,5,2]{2,0,1:T(8,128)S(1)} %add.671), channel_id=1, source_target_pairs={{0,8},{1,9},{2,10},{3,11},{4,12},{5,13},{6,14},{7,15},{8,0},{9,1},... | collective-permute-start | bytes 1928 | tf_op jit(solution)/shard_map/ppermute | solution.py:198
  176.7 18.5 %collective-permute-start.14 = (f32[1,2,1024]{2,1,0:T(2,128)}, f32[1,2,1024]{2,1,0:T(2,128)}, u32[]{:S(2)}, u32[]{:S(2)}) collective-permute-start(f32[1,2,1024]{2,1,0:T(2,128)} %stack_reshape_squeeze.39), channel_id=1, source_target_pairs={{0,1},{1,2},{2,3},{3,4},{4,5},{5,6},{6,7},{7,8},{8,9},{9,10},{10,1... | collective-permute-start | bytes 24584 | tf_op jit(solution)/shard_map/ppermute | solution.py:18
  178.6 22.5 %collective-permute-start.13 = (f32[1,2,1024]{2,1,0:T(2,128)}, f32[1,2,1024]{2,1,0:T(2,128)}, u32[]{:S(2)}, u32[]{:S(2)}) collective-permute-start(f32[1,2,1024]{2,1,0:T(2,128)} %stack_reshape_squeeze.38), channel_id=1, source_target_pairs={{1,0},{2,1},{3,2},{4,3},{5,4},{6,5},{7,6},{8,7},{9,8},{10,9},{11,1... | collective-permute-start | bytes 24584 | tf_op jit(solution)/shard_map/ppermute | solution.py:21
  235.4 16.3 %collective-permute-start.20 = (f32[257]{0:T(512)}, f32[257]{0:T(512)}, u32[]{:S(2)}, u32[]{:S(2)}) collective-permute-start(f32[257]{0:T(512)} %add.700), channel_id=1, source_target_pairs={{0,4},{1,5},{2,6},{3,7},{4,0},{5,1},{6,2},{7,3},{8,12},{9,13},{10,... | collective-permute-start | bytes 3092 | tf_op jit(solution)/shard_map/ppermute | solution.py:198
  247.0 6.6 collective-permute-start.6
  252.4 32.1 %collective-permute-start.21 = (f32[257]{0:T(512)S(1)}, f32[257]{0:T(512)S(1)}, u32[]{:S(2)}, u32[]{:S(2)}) collective-permute-start(f32[257]{0:T(512)S(1)} %add.701), channel_id=1, source_target_pairs={{0,8},{1,9},{2,10},{3,11},{4,12},{5,13},{6,14},{7,15},{8,0},{9,1},... | collective-permute-start | bytes 3092 | tf_op jit(solution)/shard_map/ppermute | solution.py:198
  332.4 28.0 %collective-permute-start.23 = (f32[1,2,1024]{2,1,0:T(2,128)}, f32[1,2,1024]{2,1,0:T(2,128)}, u32[]{:S(2)}, u32[]{:S(2)}) collective-permute-start(f32[1,2,1024]{2,1,0:T(2,128)} %stack_reshape_squeeze.41), channel_id=1, source_target_pairs={{0,1},{1,2},{2,3},{3,4},{4,5},{5,6},{6,7},{7,8},{8,9},{9,10},{10,1... | collective-permute-start | bytes 24584 | tf_op jit(solution)/shard_map/ppermute | solution.py:18
  334.9 31.4 %collective-permute-start.22 = (f32[1,2,1024]{2,1,0:T(2,128)}, f32[1,2,1024]{2,1,0:T(2,128)}, u32[]{:S(2)}, u32[]{:S(2)}) collective-permute-start(f32[1,2,1024]{2,1,0:T(2,128)} %stack_reshape_squeeze.40), channel_id=1, source_target_pairs={{1,0},{2,1},{3,2},{4,3},{5,4},{6,5},{7,6},{8,7},{9,8},{10,9},{11,1... | collective-permute-start | bytes 24584 | tf_op jit(solution)/shard_map/ppermute | solution.py:21
  444.3 13.6 %collective-permute-start.32 = (f32[1,2,1024]{2,1,0:T(2,128)S(1)}, f32[1,2,1024]{2,1,0:T(2,128)S(1)}, u32[]{:S(2)}, u32[]{:S(2)}) collective-permute-start(f32[1,2,1024]{2,1,0:T(2,128)S(1)} %stack_reshape_squeeze.43), channel_id=1, source_target_pairs={{0,1},{1,2},{2,3},{3,4},{4,5},{5,6},{6,7},{7,8},{8,9},{9,10},{10,1... | collective-permute-start | bytes 24584 | tf_op jit(solution)/shard_map/ppermute | solution.py:18
  446.3 16.3 %collective-permute-start.31 = (f32[1,2,1024]{2,1,0:T(2,128)}, f32[1,2,1024]{2,1,0:T(2,128)}, u32[]{:S(2)}, u32[]{:S(2)}) collective-permute-start(f32[1,2,1024]{2,1,0:T(2,128)} %stack_reshape_squeeze.42), channel_id=1, source_target_pairs={{1,0},{2,1},{3,2},{4,3},{5,4},{6,5},{7,6},{8,7},{9,8},{10,9},{11,1... | collective-permute-start | bytes 24584 | tf_op jit(solution)/shard_map/ppermute | solution.py:21
  492.2 7.1 collective-permute-start.38
  499.9 12.6 %collective-permute-start.39 = (f32[257]{0:T(512)}, f32[257]{0:T(512)}, u32[]{:S(2)}, u32[]{:S(2)}) collective-permute-start(f32[257]{0:T(512)} %add.733), channel_id=1, source_target_pairs={{0,8},{1,9},{2,10},{3,11},{4,12},{5,13},{6,14},{7,15},{8,0},{9,1},... | collective-permute-start | bytes 3092 | tf_op jit(solution)/shard_map/ppermute | solution.py:198
  551.6 25.7 %collective-permute-start.41 = (f32[1,2,1024]{2,1,0:T(2,128)}, f32[1,2,1024]{2,1,0:T(2,128)}, u32[]{:S(2)}, u32[]{:S(2)}) collective-permute-start(f32[1,2,1024]{2,1,0:T(2,128)} %stack_reshape_squeeze.45), channel_id=1, source_target_pairs={{0,1},{1,2},{2,3},{3,4},{4,5},{5,6},{6,7},{7,8},{8,9},{9,10},{10,1... | collective-permute-start | bytes 24584 | tf_op jit(solution)/shard_map/ppermute | solution.py:18
  554.1 29.1 %collective-permute-start.40 = (f32[1,2,1024]{2,1,0:T(2,128)}, f32[1,2,1024]{2,1,0:T(2,128)}, u32[]{:S(2)}, u32[]{:S(2)}) collective-permute-start(f32[1,2,1024]{2,1,0:T(2,128)} %stack_reshape_squeeze.44), channel_id=1, source_target_pairs={{1,0},{2,1},{3,2},{4,3},{5,4},{6,5},{7,6},{8,7},{9,8},{10,9},{11,1... | collective-permute-start | bytes 24584 | tf_op jit(solution)/shard_map/ppermute | solution.py:21
  672.8 12.3 %collective-permute-start.50 = (f32[1,2,1024]{2,1,0:T(2,128)S(1)}, f32[1,2,1024]{2,1,0:T(2,128)S(1)}, u32[]{:S(2)}, u32[]{:S(2)}) collective-permute-start(f32[1,2,1024]{2,1,0:T(2,128)S(1)} %stack_reshape_squeeze.47), channel_id=1, source_target_pairs={{0,1},{1,2},{2,3},{3,4},{4,5},{5,6},{6,7},{7,8},{8,9},{9,10},{10,1... | collective-permute-start | bytes 24584 | tf_op jit(solution)/shard_map/ppermute | solution.py:18
  675.2 14.0 %collective-permute-start.49 = (f32[1,2,1024]{2,1,0:T(2,128)}, f32[1,2,1024]{2,1,0:T(2,128)}, u32[]{:S(2)}, u32[]{:S(2)}) collective-permute-start(f32[1,2,1024]{2,1,0:T(2,128)} %stack_reshape_squeeze.46), channel_id=1, source_target_pairs={{1,0},{2,1},{3,2},{4,3},{5,4},{6,5},{7,6},{8,7},{9,8},{10,9},{11,1... | collective-permute-start | bytes 24584 | tf_op jit(solution)/shard_map/ppermute | solution.py:21
  713.5 23.9 %collective-permute-start.55 = (f32[257]{0:T(512)S(1)}, f32[257]{0:T(512)S(1)}, u32[]{:S(2)}, u32[]{:S(2)}) collective-permute-start(f32[257]{0:T(512)S(1)} %add.759), channel_id=1, source_target_pairs={{0,2},{1,3},{2,0},{3,1},{4,6},{5,7},{6,4},{7,5},{8,10},{9,11},{10,... | collective-permute-start | bytes 3092 | tf_op jit(solution)/shard_map/ppermute | solution.py:198
  738.0 12.3 %collective-permute-start.56 = (f32[257]{0:T(512)}, f32[257]{0:T(512)}, u32[]{:S(2)}, u32[]{:S(2)}) collective-permute-start(f32[257]{0:T(512)} %add.760), channel_id=1, source_target_pairs={{0,4},{1,5},{2,6},{3,7},{4,0},{5,1},{6,2},{7,3},{8,12},{9,13},{10,... | collective-permute-start | bytes 3092 | tf_op jit(solution)/shard_map/ppermute | solution.py:198
  751.7 35.1 %collective-permute-start.57 = (f32[257]{0:T(512)}, f32[257]{0:T(512)}, u32[]{:S(2)}, u32[]{:S(2)}) collective-permute-start(f32[257]{0:T(512)} %add.761), channel_id=1, source_target_pairs={{0,8},{1,9},{2,10},{3,11},{4,12},{5,13},{6,14},{7,15},{8,0},{9,1},... | collective-permute-start | bytes 3092 | tf_op jit(solution)/shard_map/ppermute | solution.py:198
  (261 other events, 2096.1 us)
where the time goes:
time: 810 us; the launch traced here: 796 us
  local copies, waits for them, and re-layouts  344 us (42%)
  other arithmetic  145 us (18%)
  starting transfers between devices  145 us (18%)
  blocking collectives  78.8 us (10%)
  waiting for transfers between devices  54 us (7%)
  between operations  25.7 us (3%)
    ppermute x46, starting transfers between devices, butterfly(): values = values + lax.ppermute(values, axis, pairs)  124 us
    all_gather x6, blocking collectives, apply_operator(): portion = lax.all_gather(outgoing_sides[None], 'brick', axis=0, tiled=True)  78.8 us
    ppermute x46, waiting for transfers between devices, butterfly(): values = values + lax.ppermute(values, axis, pairs)  54 us
    broadcast_in_dim x26, local copies, waits for them, and re-layouts, apply_operator(): jnp.where(cube_third == BS - 1, from_above, jnp.roll(cube, -1, axis=3))  46.7 us
    broadcast_in_dim x26, local copies, waits for them, and re-layouts, apply_operator(): jnp.where(cube_third == 0, from_below, jnp.roll(cube, 1, axis=3))  42.9 us
    concatenate x12, local copies, waits for them, and re-layouts, apply_operator(): jnp.roll(cube, 1, axis=3)  25.5 us
    concatenate x12, local copies, waits for them, and re-layouts, apply_operator(): jnp.roll(cube, -1, axis=3)  23 us
    concatenate x15, local copies, waits for them, and re-layouts, apply_operator(): jnp.concatenate([field[:, :, BS:], beyond_yplus], axis=2)  21.9 us
  transfers between devices with their start and end apart: 58, of which 34 were waited for; matrix products, arithmetic and copies ran while one was open for 30% of the time, Pallas kernels for 0%

commit v1 on v0

--- a/solution.py
+++ b/solution.py
@@ -119,7 +119,9 @@
                 pad_rows(grid_upper_y[:, PATCH_Y - 1], capacity),
             ]
         )
-        portion = lax.all_gather(outgoing_sides[None], "brick", axis=0, tiled=True)
+        part = outgoing_sides[None]
+        sent = jnp.stack([part] * lax.axis_size("brick"))
+        portion = jnp.concatenate(lax.all_to_all(sent, "brick", 0, 0), axis=0)
         sources = jnp.arange(portion.shape[0], dtype=jnp.int32)
         matches = sources[:, None] == wanted[None, :]
         remote = jnp.zeros((4, capacity, face_size), jnp.float32) + jnp.sum(

time: 810 us -> 758 us (0.936)
  blocking collectives: 78.8 us -> 0 us
  starting transfers between devices: 145 us -> 188 us
  local copies, waits for them, and re-layouts: 344 us -> 329 us
  waiting for transfers between devices: 54 us -> 42.6 us
  other arithmetic: 145 us -> 154 us
    all_gather x6 -> x0, blocking collectives: 78.8 us -> none  [apply_operator(): portion = lax.all_gather(outgoing_sides[None], 'brick', axis=0, tiled=True)]
    all_to_all x0 -> x6, starting transfers between devices: none -> 28.6 us  [apply_operator(): portion = jnp.concatenate(lax.all_to_all(sent, 'brick', 0, 0), axis=0)]
    ppermute x46, starting transfers between devices: 124 us -> 139 us  [butterfly(): values = values + lax.ppermute(values, axis, pairs)]
    ppermute x46, waiting for transfers between devices: 54 us -> 42.6 us  [butterfly(): values = values + lax.ppermute(values, axis, pairs)]
    another operation x0 -> x19, local copies, waits for them, and re-layouts: none -> 11.4 us  [the longest x6 4.7 us: apply_operator(): sent = jnp.stack([part] * lax.axis_size('brick'))]
    concatenate x14 -> x24, local copies, waits for them, and re-layouts: 20.6 us -> 25.5 us  [apply_operator(): jnp.concatenate([field[:, 1:, :], beyond_xplus[:, None, :]], axis=1)]
    concatenate x11 -> x18, local copies, waits for them, and re-layouts: 18.3 us -> 21.5 us  [apply_operator(): jnp.concatenate([beyond_xminus[:, None, :], field[:, :-1, :]], axis=1)]
  transfers between devices with their start and end apart: 58 -> 64, of which waited for: 34 -> 34; matrix products, arithmetic and copies ran while one was open for 30% -> 37% of each run, Pallas kernels for 0% -> 0%
where the time goes in v1:
time: 758 us; the launch traced here: 743 us
  local copies, waits for them, and re-layouts  329 us (43%)
  starting transfers between devices  188 us (25%)
  other arithmetic  154 us (20%)
  waiting for transfers between devices  42.6 us (6%)
  between operations  26.1 us (3%)
    ppermute x46, starting transfers between devices, butterfly(): values = values + lax.ppermute(values, axis, pairs)  139 us
    ppermute x46, waiting for transfers between devices, butterfly(): values = values + lax.ppermute(values, axis, pairs)  42.6 us
    broadcast_in_dim x26, local copies, waits for them, and re-layouts, apply_operator(): jnp.where(cube_third == BS - 1, from_above, jnp.roll(cube, -1, axis=3))  41.1 us
    broadcast_in_dim x26, local copies, waits for them, and re-layouts, apply_operator(): jnp.where(cube_third == 0, from_below, jnp.roll(cube, 1, axis=3))  40.3 us
    all_to_all x6, starting transfers between devices, apply_operator(): portion = jnp.concatenate(lax.all_to_all(sent, 'brick', 0, 0), axis=0)  28.6 us
    concatenate x24, local copies, waits for them, and re-layouts, apply_operator(): jnp.concatenate([field[:, 1:, :], beyond_xplus[:, None, :]], axis=1)  25.5 us
    concatenate x12, local copies, waits for them, and re-layouts, apply_operator(): jnp.roll(cube, -1, axis=3)  24.2 us
    concatenate x12, local copies, waits for them, and re-layouts, apply_operator(): jnp.roll(cube, 1, axis=3)  24.2 us
  transfers between devices with their start and end apart: 64, of which 34 were waited for; matrix products, arithmetic and copies ran while one was open for 37% of the time, Pallas kernels for 0%

profile of v1, /device:TPU:0, one launch (start us, length us, event | category | flops | bytes accessed | tf_op | source)
XLA Modules:
  0.0 743.1 jit_solution(3721875262939553294)
XLA Ops:
  10.9 4.6 all-to-all-start
  42.1 5.5 multiply_divide_fusion.2
  71.6 5.6 collective-permute-start.3
  119.4 8.4 %fusion.46 = (f32[2,32,32,32]{3,2,1,0:T(8,128)S(1)}, f32[2,32,32,32]{3,2,1,0:T(8,128)}, f32[2,32,32,32]{3,2,1,0:T(8,128)}) fusion(f32[2,32,32,32]{3,2,1,0:T(8,128)} %get-tuple-element.67, f32[2,32,32,32]{3,2,1,0:T(8,128)} %copy-done.17, f32[2,32,32,32]{3,2,1,0:T(8,128)} %copy-done.16, f32[2,32,32,32]{3,2,1,0:T(8,128)} %concatenate.668, ...), kind=kLoop, calls=%fused_computation.88 | loop fusion | flops 2293760 | bytes 4538480 | tf_op jit(solution)/shard_map/add | solution.py:233
  150.2 4.8 all-to-all-start.1
  219.6 4.7 collective-permute-start.20
  244.7 4.9 collective-permute-start.8
  279.0 6.6 multiply_divide_fusion.1
  300.3 4.8 all-to-all-start.2
  363.8 4.7 collective-permute-start.26
  380.3 5.2 collective-permute-start.29
  386.5 4.7 collective-permute-start.30
  396.1 6.4 multiply_add_fusion.1
  408.0 4.8 all-to-all-start.3
  460.0 5.5 collective-permute-start.38
  486.7 6.2 multiply_divide_fusion
  504.2 4.8 all-to-all-start.4
  565.9 4.7 collective-permute-start.44
  581.9 5.9 collective-permute-start.47
  588.6 4.4 collective-permute-start.48
  598.3 9.3 %multiply_add_fusion = f32[2,32,32,32]{3,2,1,0:T(8,128)S(1)} fusion(f32[2,32,32,32]{3,2,1,0:T(8,128)} %copy-done.18, f32[2,32,32,32]{3,2,1,0:T(8,128)} %get-tuple-element.67, f32[2,32,32,32]{3,2,1,0:T(8,128)} %copy-done.17, f32[2,32,32,32]{3,2,1,0:T(8,128)} %copy-done.16, f32[2,32,32,32]{3,2,1,0:T(8,128)} %concatenate.784, ...), kind=kLoop, calls=%fused_computation.76 | loop fusion | flops 3735552 | bytes 5865592 | tf_op jit(solution)/shard_map/add | solution.py:265
  613.4 4.8 all-to-all-start.5
  677.2 4.2 collective-permute-start.55
  736.2 5.8 fusion.148
  (982 shorter events, 585.8 us)
Async XLA Ops:
  10.9 99.4 %all-to-all-start = ((f32[8,1,4,2,1024]{4,3,2,1,0:T(2,128)}), f32[8,1,4,2,1024]{4,3,2,1,0:T(2,128)}, u32[]{:S(2)}, u32[]{:S(2)}) async-start(f32[8,1,4,2,1024]{4,3,2,1,0:T(2,128)} %stack.143), calls=%async_computation | async-start | bytes 524288 | tf_op jit(solution)/shard_map/all_to_all | solution.py:124
  51.3 19.4 %collective-permute-start.2 = (f32[16,5,2]{2,0,1:T(8,128)}, f32[16,5,2]{2,0,1:T(8,128)}, u32[]{:S(2)}, u32[]{:S(2)}) collective-permute-start(f32[16,5,2]{2,0,1:T(8,128)} %broadcast_multiply_fusion.3), channel_id=1, source_target_pairs={{0,1},{1,0},{2,3},{3,2},{4,5},{5,4},{6,7},{7,6},{8,9},{9,8},{10,11... | collective-permute-start | bytes 1928 | tf_op jit(solution)/shard_map/ppermute | solution.py:200
  57.0 47.3 %collective-permute-start.1 = (f32[1,2,1024]{2,1,0:T(2,128)}, f32[1,2,1024]{2,1,0:T(2,128)}, u32[]{:S(2)}, u32[]{:S(2)}) collective-permute-start(f32[1,2,1024]{2,1,0:T(2,128)} %stack_reshape_squeeze.37), channel_id=1, source_target_pairs={{0,1},{1,2},{2,3},{3,4},{4,5},{5,6},{6,7},{7,8},{8,9},{9,10},{10,1... | collective-permute-start | bytes 24584 | tf_op jit(solution)/shard_map/ppermute | solution.py:18
  61.0 40.7 %collective-permute-start = (f32[1,2,1024]{2,1,0:T(2,128)}, f32[1,2,1024]{2,1,0:T(2,128)}, u32[]{:S(2)}, u32[]{:S(2)}) collective-permute-start(f32[1,2,1024]{2,1,0:T(2,128)} %stack_reshape_squeeze.36), channel_id=1, source_target_pairs={{1,0},{2,1},{3,2},{4,3},{5,4},{6,5},{7,6},{8,7},{9,8},{10,9},{11,1... | collective-permute-start | bytes 24584 | tf_op jit(solution)/shard_map/ppermute | solution.py:21
  150.2 32.0 %all-to-all-start.1 = ((f32[8,1,4,2,1024]{4,3,2,1,0:T(2,128)}), f32[8,1,4,2,1024]{4,3,2,1,0:T(2,128)}, u32[]{:S(2)}, u32[]{:S(2)}) async-start(f32[8,1,4,2,1024]{4,3,2,1,0:T(2,128)} %stack.151), calls=%async_computation.1 | async-start | bytes 524288 | tf_op jit(solution)/shard_map/all_to_all | solution.py:124
  157.9 12.6 %collective-permute-start.14 = (f32[1,2,1024]{2,1,0:T(2,128)}, f32[1,2,1024]{2,1,0:T(2,128)}, u32[]{:S(2)}, u32[]{:S(2)}) collective-permute-start(f32[1,2,1024]{2,1,0:T(2,128)} %stack_reshape_squeeze.39), channel_id=1, source_target_pairs={{0,1},{1,2},{2,3},{3,4},{4,5},{5,6},{6,7},{7,8},{8,9},{9,10},{10,1... | collective-permute-start | bytes 24584 | tf_op jit(solution)/shard_map/ppermute | solution.py:18
  159.8 16.6 %collective-permute-start.13 = (f32[1,2,1024]{2,1,0:T(2,128)}, f32[1,2,1024]{2,1,0:T(2,128)}, u32[]{:S(2)}, u32[]{:S(2)}) collective-permute-start(f32[1,2,1024]{2,1,0:T(2,128)} %stack_reshape_squeeze.38), channel_id=1, source_target_pairs={{1,0},{2,1},{3,2},{4,3},{5,4},{6,5},{7,6},{8,7},{9,8},{10,9},{11,1... | collective-permute-start | bytes 24584 | tf_op jit(solution)/shard_map/ppermute | solution.py:21
  219.6 16.6 %collective-permute-start.20 = (f32[257]{0:T(512)}, f32[257]{0:T(512)}, u32[]{:S(2)}, u32[]{:S(2)}) collective-permute-start(f32[257]{0:T(512)} %add.700), channel_id=1, source_target_pairs={{0,4},{1,5},{2,6},{3,7},{4,0},{5,1},{6,2},{7,3},{8,12},{9,13},{10,... | collective-permute-start | bytes 3092 | tf_op jit(solution)/shard_map/ppermute | solution.py:200
  237.0 34.4 %collective-permute-start.21 = (f32[257]{0:T(512)S(1)}, f32[257]{0:T(512)S(1)}, u32[]{:S(2)}, u32[]{:S(2)}) collective-permute-start(f32[257]{0:T(512)S(1)} %add.701), channel_id=1, source_target_pairs={{0,8},{1,9},{2,10},{3,11},{4,12},{5,13},{6,14},{7,15},{8,0},{9,1},... | collective-permute-start | bytes 3092 | tf_op jit(solution)/shard_map/ppermute | solution.py:200
  300.3 37.6 %all-to-all-start.2 = ((f32[8,1,4,2,1024]{4,3,2,1,0:T(2,128)}), f32[8,1,4,2,1024]{4,3,2,1,0:T(2,128)}, u32[]{:S(2)}, u32[]{:S(2)}) async-start(f32[8,1,4,2,1024]{4,3,2,1,0:T(2,128)} %stack.157), calls=%async_computation.2 | async-start | bytes 524288 | tf_op jit(solution)/shard_map/all_to_all | solution.py:124
  308.0 18.2 %collective-permute-start.23 = (f32[1,2,1024]{2,1,0:T(2,128)}, f32[1,2,1024]{2,1,0:T(2,128)}, u32[]{:S(2)}, u32[]{:S(2)}) collective-permute-start(f32[1,2,1024]{2,1,0:T(2,128)} %stack_reshape_squeeze.41), channel_id=1, source_target_pairs={{0,1},{1,2},{2,3},{3,4},{4,5},{5,6},{6,7},{7,8},{8,9},{9,10},{10,1... | collective-permute-start | bytes 24584 | tf_op jit(solution)/shard_map/ppermute | solution.py:18
  310.5 21.5 %collective-permute-start.22 = (f32[1,2,1024]{2,1,0:T(2,128)}, f32[1,2,1024]{2,1,0:T(2,128)}, u32[]{:S(2)}, u32[]{:S(2)}) collective-permute-start(f32[1,2,1024]{2,1,0:T(2,128)} %stack_reshape_squeeze.40), channel_id=1, source_target_pairs={{1,0},{2,1},{3,2},{4,3},{5,4},{6,5},{7,6},{8,7},{9,8},{10,9},{11,1... | collective-permute-start | bytes 24584 | tf_op jit(solution)/shard_map/ppermute | solution.py:21
  408.0 24.3 %all-to-all-start.3 = ((f32[8,1,4,2,1024]{4,3,2,1,0:T(2,128)}), f32[8,1,4,2,1024]{4,3,2,1,0:T(2,128)}, u32[]{:S(2)}, u32[]{:S(2)}) async-start(f32[8,1,4,2,1024]{4,3,2,1,0:T(2,128)} %stack.163), calls=%async_computation.3 | async-start | bytes 524288 | tf_op jit(solution)/shard_map/all_to_all | solution.py:124
  413.6 11.2 %collective-permute-start.32 = (f32[1,2,1024]{2,1,0:T(2,128)S(1)}, f32[1,2,1024]{2,1,0:T(2,128)S(1)}, u32[]{:S(2)}, u32[]{:S(2)}) collective-permute-start(f32[1,2,1024]{2,1,0:T(2,128)S(1)} %stack_reshape_squeeze.43), channel_id=1, source_target_pairs={{0,1},{1,2},{2,3},{3,4},{4,5},{5,6},{6,7},{7,8},{8,9},{9,10},{10,1... | collective-permute-start | bytes 24584 | tf_op jit(solution)/shard_map/ppermute | solution.py:18
  415.8 12.0 %collective-permute-start.31 = (f32[1,2,1024]{2,1,0:T(2,128)}, f32[1,2,1024]{2,1,0:T(2,128)}, u32[]{:S(2)}, u32[]{:S(2)}) collective-permute-start(f32[1,2,1024]{2,1,0:T(2,128)} %stack_reshape_squeeze.42), channel_id=1, source_target_pairs={{1,0},{2,1},{3,2},{4,3},{5,4},{6,5},{7,6},{8,7},{9,8},{10,9},{11,1... | collective-permute-start | bytes 24584 | tf_op jit(solution)/shard_map/ppermute | solution.py:21
  467.7 12.5 %collective-permute-start.39 = (f32[257]{0:T(512)}, f32[257]{0:T(512)}, u32[]{:S(2)}, u32[]{:S(2)}) collective-permute-start(f32[257]{0:T(512)} %add.733), channel_id=1, source_target_pairs={{0,8},{1,9},{2,10},{3,11},{4,12},{5,13},{6,14},{7,15},{8,0},{9,1},... | collective-permute-start | bytes 3092 | tf_op jit(solution)/shard_map/ppermute | solution.py:200
  504.2 35.7 %all-to-all-start.4 = ((f32[8,1,4,2,1024]{4,3,2,1,0:T(2,128)}), f32[8,1,4,2,1024]{4,3,2,1,0:T(2,128)}, u32[]{:S(2)}, u32[]{:S(2)}) async-start(f32[8,1,4,2,1024]{4,3,2,1,0:T(2,128)} %stack.169), calls=%async_computation.4 | async-start | bytes 524288 | tf_op jit(solution)/shard_map/all_to_all | solution.py:124
  511.3 17.6 %collective-permute-start.41 = (f32[1,2,1024]{2,1,0:T(2,128)S(1)}, f32[1,2,1024]{2,1,0:T(2,128)S(1)}, u32[]{:S(2)}, u32[]{:S(2)}) collective-permute-start(f32[1,2,1024]{2,1,0:T(2,128)S(1)} %stack_reshape_squeeze.45), channel_id=1, source_target_pairs={{0,1},{1,2},{2,3},{3,4},{4,5},{5,6},{6,7},{7,8},{8,9},{9,10},{10,1... | collective-permute-start | bytes 24584 | tf_op jit(solution)/shard_map/ppermute | solution.py:18
  513.2 20.9 %collective-permute-start.40 = (f32[1,2,1024]{2,1,0:T(2,128)}, f32[1,2,1024]{2,1,0:T(2,128)}, u32[]{:S(2)}, u32[]{:S(2)}) collective-permute-start(f32[1,2,1024]{2,1,0:T(2,128)} %stack_reshape_squeeze.44), channel_id=1, source_target_pairs={{1,0},{2,1},{3,2},{4,3},{5,4},{6,5},{7,6},{8,7},{9,8},{10,9},{11,1... | collective-permute-start | bytes 24584 | tf_op jit(solution)/shard_map/ppermute | solution.py:21
  613.4 21.8 %all-to-all-start.5 = ((f32[8,1,4,2,1024]{4,3,2,1,0:T(2,128)}), f32[8,1,4,2,1024]{4,3,2,1,0:T(2,128)}, u32[]{:S(2)}, u32[]{:S(2)}) async-start(f32[8,1,4,2,1024]{4,3,2,1,0:T(2,128)} %stack.175), calls=%async_computation.5 | async-start | bytes 524288 | tf_op jit(solution)/shard_map/all_to_all | solution.py:124
  620.3 11.1 %collective-permute-start.49 = (f32[1,2,1024]{2,1,0:T(2,128)S(1)}, f32[1,2,1024]{2,1,0:T(2,128)S(1)}, u32[]{:S(2)}, u32[]{:S(2)}) collective-permute-start(f32[1,2,1024]{2,1,0:T(2,128)S(1)} %stack_reshape_squeeze.46), channel_id=1, source_target_pairs={{1,0},{2,1},{3,2},{4,3},{5,4},{6,5},{7,6},{8,7},{9,8},{10,9},{11,1... | collective-permute-start | bytes 24584 | tf_op jit(solution)/shard_map/ppermute | solution.py:21
  654.5 22.7 %collective-permute-start.54 = (f32[257]{0:T(512)S(1)}, f32[257]{0:T(512)S(1)}, u32[]{:S(2)}, u32[]{:S(2)}) collective-permute-start(f32[257]{0:T(512)S(1)} %add.758), channel_id=1, source_target_pairs={{0,1},{1,0},{2,3},{3,2},{4,5},{5,4},{6,7},{7,6},{8,9},{9,8},{10,11... | collective-permute-start | bytes 3092 | tf_op jit(solution)/shard_map/ppermute | solution.py:200
  685.9 23.5 %collective-permute-start.56 = (f32[257]{0:T(512)}, f32[257]{0:T(512)}, u32[]{:S(2)}, u32[]{:S(2)}) collective-permute-start(f32[257]{0:T(512)} %add.760), channel_id=1, source_target_pairs={{0,4},{1,5},{2,6},{3,7},{4,0},{5,1},{6,2},{7,3},{8,12},{9,13},{10,... | collective-permute-start | bytes 3092 | tf_op jit(solution)/shard_map/ppermute | solution.py:200
  710.7 23.5 %collective-permute-start.57 = (f32[257]{0:T(512)}, f32[257]{0:T(512)}, u32[]{:S(2)}, u32[]{:S(2)}) collective-permute-start(f32[257]{0:T(512)} %add.761), channel_id=1, source_target_pairs={{0,8},{1,9},{2,10},{3,11},{4,12},{5,13},{6,14},{7,15},{8,0},{9,1},... | collective-permute-start | bytes 3092 | tf_op jit(solution)/shard_map/ppermute | solution.py:200
  (257 other events, 1919.5 us)
